TPU v7x, 256 devices: a whole 4x4x8 slice. The times are simulated.
256 devices in a mesh: dp: 2 (over core), row: 16 (over x, y), col: 8 (over z).
Axes of the slice: x: 4, y: 4, z: 8, core: 2. Of those that a mesh axis runs over, the one named last changes fastest.
Arguments:
- tokens: bfloat16 [768, 8192], P(('dp', 'col'), 'row'), may hold values from -160 to 160
- norm_gain: float32 [8192], P('row'), may hold values from 0.3 to 3
- gate_weight: bfloat16 [8192, 14336], P('row', ('dp', 'col')), may hold values from -0.0625 to 0.0625
- up_weight: bfloat16 [8192, 14336], P('row', ('dp', 'col')), may hold values from -0.0625 to 0.0625
- down_weight: bfloat16 [14336, 8192], P(('dp', 'col'), 'row'), may hold values from -0.046875 to 0.046875
- gate_keep: int32 [64, 112], P('row', ('dp', 'col')), may hold values from 0 to 1, as said below
- up_keep: int32 [64, 112], P('row', ('dp', 'col')), may hold values from 0 to 1, as said below
- down_keep: int32 [112, 64], P(('dp', 'col'), 'row'), may hold values from 0 to 1, as said below
- cotangent: bfloat16 [768, 8192], P(('dp', 'col'), 'row'), may hold values from -80 to 80
Outputs:
- branch: bfloat16 [768, 8192], P(('dp', 'col'), 'row')
- grad_tokens: float32 [768, 8192], P(('dp', 'col'), 'row')
- grad_gain: float32 [8192], P('row')
- grad_gate: float32 [8192, 14336], P('row', ('dp', 'col'))
- grad_up: float32 [8192, 14336], P('row', ('dp', 'col'))
- grad_down: float32 [14336, 8192], P(('dp', 'col'), 'row')
Inputs may be any that keep to these rules, and one draw needn't show every extreme that they name: `gate_keep`: 1 keeps a 128 x 128 block of the gate projection, 0 prunes it. `up_keep`: 1 keeps a 128 x 128 block of the up projection, 0 prunes it. `down_keep`: 1 keeps a 128 x 128 block of the down projection, 0 prunes it.
All inputs are finite; a program needn't handle non-finite values.
Results may differ from a plain program's by a relative error of at most 0.0065.
Values may be sent and summed in bfloat16 or wider, within the bound.
A program may use at most 128 MiB of HBM per device.

v0:
```python
import jax
import jax.numpy as jnp
from jax import lax
from jax.sharding import PartitionSpec as P

D = 8192
BLOCK = 128


def expand_keep(keep, target_type):
    return jnp.repeat(jnp.repeat(keep, BLOCK, axis=0), BLOCK, axis=1).astype(target_type)


def activate(gate, up_value):
    return (gate * jax.nn.sigmoid(gate) * up_value).astype(jnp.bfloat16)


def on_device(
    tokens, norm_gain, gate_weight, up_weight, down_weight, gate_keep, up_keep, down_keep, cotangent
):
    token_f = tokens.astype(jnp.float32)
    square = lax.psum(jnp.sum(token_f * token_f, axis=1), "row")
    inv_rms = lax.rsqrt(square[:, None] / D + 1e-05)
    normed = (token_f * inv_rms * norm_gain).astype(jnp.bfloat16)
    gate_masked = gate_weight * expand_keep(gate_keep, jnp.bfloat16)
    up_masked = up_weight * expand_keep(up_keep, jnp.bfloat16)
    down_masked = down_weight * expand_keep(down_keep, jnp.bfloat16)
    gate_full, up_full = (
        lax.all_gather(gate_masked, "dp", axis=1, tiled=True),
        lax.all_gather(up_masked, "dp", axis=1, tiled=True),
    )
    down_full = lax.all_gather(down_masked, "dp", axis=0, tiled=True)
    seen_rows = lax.all_gather(normed, "col", axis=0, tiled=True)
    seen_cot = lax.all_gather(cotangent, "col", axis=0, tiled=True)
    width_f = gate_full.shape[1]
    contract_last = (((1,), (1,)), ((), ()))
    contract_first = (((0,), (0,)), ((), ()))
    row_block = seen_rows
    summed = lax.psum_scatter(
        jnp.concatenate(
            [
                jnp.dot(row_block, gate_full, preferred_element_type=jnp.float32),
                jnp.dot(row_block, up_full, preferred_element_type=jnp.float32),
            ],
            axis=1,
        ),
        "row",
        scatter_dimension=0,
        tiled=True,
    )
    gate_part = summed[:, :width_f]
    up_part = summed[:, width_f:]
    hidden = lax.all_gather(activate(gate_part, up_part), "row", axis=0, tiled=True)
    row_block = hidden
    branch_sum = lax.psum_scatter(
        jnp.dot(row_block, down_full, preferred_element_type=jnp.float32),
        "col",
        scatter_dimension=0,
        tiled=True,
    )
    branch = branch_sum.astype(jnp.bfloat16)
    row_block = seen_cot
    hidden_grad = lax.psum_scatter(
        lax.dot_general(row_block, down_full, contract_last, preferred_element_type=jnp.float32),
        "row",
        scatter_dimension=0,
        tiled=True,
    )
    sigmoid_gate = jax.nn.sigmoid(gate_part)
    gate_grad = (
        hidden_grad * up_part * sigmoid_gate * (1.0 + gate_part * (1.0 - sigmoid_gate))
    ).astype(jnp.bfloat16)
    up_grad = (hidden_grad * gate_part * sigmoid_gate).astype(jnp.bfloat16)
    gate_grads, up_grads = (
        lax.all_gather(gate_grad, "row", axis=0, tiled=True),
        lax.all_gather(up_grad, "row", axis=0, tiled=True),
    )
    normed_grad = lax.psum_scatter(
        lax.dot_general(gate_grads, gate_full, contract_last, preferred_element_type=jnp.float32)
        + lax.dot_general(up_grads, up_full, contract_last, preferred_element_type=jnp.float32),
        "col",
        scatter_dimension=0,
        tiled=True,
    )
    down_local = lax.dot_general(
        hidden, seen_cot, contract_first, preferred_element_type=jnp.float32
    )
    gate_local = lax.dot_general(
        seen_rows, gate_grads, contract_first, preferred_element_type=jnp.float32
    )
    up_local = lax.dot_general(
        seen_rows, up_grads, contract_first, preferred_element_type=jnp.float32
    )
    gate_total, up_total = (
        lax.psum_scatter(gate_local, "dp", scatter_dimension=1, tiled=True),
        lax.psum_scatter(up_local, "dp", scatter_dimension=1, tiled=True),
    )
    down_total = lax.psum_scatter(down_local, "dp", scatter_dimension=0, tiled=True)
    grad_gate = gate_total * expand_keep(gate_keep, jnp.float32)
    grad_up = up_total * expand_keep(up_keep, jnp.float32)
    grad_down = down_total * expand_keep(down_keep, jnp.float32)
    grad_gain = lax.psum(jnp.sum(normed_grad * token_f * inv_rms, axis=0), ("dp", "col"))
    inner_dot = lax.psum(jnp.sum(norm_gain * normed_grad * token_f, axis=1), "row")
    grad_tokens = (
        inv_rms * norm_gain * normed_grad
        - token_f * inv_rms * inv_rms * inv_rms * inner_dot[:, None] / D
    )
    return (branch, grad_tokens, grad_gain, grad_gate, grad_up, grad_down)


def solution(mesh):
    in_specs = (
        P(("dp", "col"), "row"),
        P("row"),
        P("row", ("dp", "col")),
        P("row", ("dp", "col")),
        P(("dp", "col"), "row"),
        P("row", ("dp", "col")),
        P("row", ("dp", "col")),
        P(("dp", "col"), "row"),
        P(("dp", "col"), "row"),
    )
    out_specs = (
        P(("dp", "col"), "row"),
        P(("dp", "col"), "row"),
        P("row"),
        P("row", ("dp", "col")),
        P("row", ("dp", "col")),
        P(("dp", "col"), "row"),
    )
    return jax.shard_map(
        on_device, mesh=mesh, in_specs=in_specs, out_specs=out_specs, check_vma=False
    )
```

profile of v0, /device:TPU:1, one launch (start us, length us, event | category | flops | bytes accessed | tf_op | source)
XLA Modules:
  0.0 618.9 jit_solution(13454673228477233298)
XLA Ops:
  7.2 0.8 fusion.13
  8.2 1.5 copy.30
  9.7 1.0 bitcast_multiply_fusion.3
  11.2 0.5 copy.32
  11.7 1.0 bitcast_multiply_fusion.2
  12.9 1.1 broadcast_in_dim.46
  14.1 1.1 bitcast_multiply_fusion.1
  15.4 34.2 %psum.21 = f32[48]{0:T(128)S(1)} all-reduce(f32[48]{0:T(128)S(1)} %fusion.7), channel_id=1, replica_groups=mesh['dp'=2,'row'=16,'col'=8] {'row'}, use_global_device_ids=true, to_apply=%region_1.0 | all-reduce | flops 48 | bytes 384 | tf_op jit(solution)/shard_map/psum | solution.py:22
  49.6 0.6 copy-done.12
  50.3 22.6 %all_gather.24 = bf16[384,512]{1,0:T(8,128)(2,1)S(1)} all-gather(bf16[48,512]{1,0:T(8,128)(2,1)S(1)} %fusion.2), channel_id=1, replica_groups=mesh['dp'=2,'row'=16,'col'=8] {'col'}, dimensions={0}, use_global_device_ids=true | all-gather | bytes 442368 | tf_op jit(solution)/shard_map/all_gather | solution.py:33
  72.9 2.4 fusion.14
  75.3 2.4 fusion.15
  77.7 3.2 pad_maximum_fusion
  81.0 0.7 copy-done.10
  81.7 19.5 %all_gather.29 = bf16[384,512]{1,0:T(8,128)(2,1)S(1)} all-gather(bf16[48,512]{1,0:T(8,128)(2,1)S(1)} %copy-done.10), channel_id=1, replica_groups=mesh['dp'=2,'row'=16,'col'=8] {'col'}, dimensions={0}, use_global_device_ids=true | all-gather | bytes 442368 | tf_op jit(solution)/shard_map/all_gather | solution.py:34
  101.3 2.6 convolution_bitcast_fusion
  103.9 2.3 copy.34
  106.3 0.6 copy-done.16
  106.9 0.6 dynamic-slice
  108.1 105.8 %all-reduce.4.cloned.1.call-done = f32[384,3584]{1,0:T(8,128)} async-done(((f32[384,3584]{1,0:T(8,128)}), f32[384,3584]{1,0:T(8,128)}) %all-reduce.4.cloned.1.call-update) | async-done | bytes 5505040
  213.9 83.0 %reduce-scatter.19.cloned.1.call-done = f32[24,1792]{1,0:T(8,128)} async-done(((f32[384,1792]{1,0:T(8,128)}), f32[24,1792]{1,0:T(8,128)}) %reduce-scatter.19.cloned.1.call-update) | async-done | bytes 172048
  297.0 1.9 multiply_convert_fusion
  298.9 0.7 all-gather.15.cloned.1.call-update
  299.7 0.7 all-gather.17.cloned.1.call-update
  300.4 46.9 %all-gather.11.cloned.1.call-done = bf16[384,1792]{1,0:T(8,128)(2,1)} async-done(((bf16[24,1792]{1,0:T(8,128)(2,1)}), bf16[384,1792]{1,0:T(8,128)(2,1)}) %all-gather.11.cloned.1.call-update) | async-done | bytes 1376272 | tf_op jit(solution)/shard_map/all_gather | solution.py:53
  347.3 3.1 fusion.16
  350.5 47.7 %all-gather.15.cloned.1.call-done = bf16[384,1792]{1,0:T(8,128)(2,1)} async-done(((bf16[24,1792]{1,0:T(8,128)(2,1)}), bf16[384,1792]{1,0:T(8,128)(2,1)}) %all-gather.15.cloned.1.call-update) | async-done | bytes 1376272 | tf_op jit(solution)/shard_map/all_gather | solution.py:75
  398.2 2.8 fusion.17
  401.0 48.1 %all-gather.17.cloned.1.call-done = bf16[384,1792]{1,0:T(8,128)(2,1)} async-done(((bf16[24,1792]{1,0:T(8,128)(2,1)}), bf16[384,1792]{1,0:T(8,128)(2,1)}) %all-gather.17.cloned.1.call-update) | async-done | bytes 1376272 | tf_op jit(solution)/shard_map/all_gather | solution.py:76
  449.1 3.1 convolution_add_fusion
  452.3 4.3 fusion.18
  456.6 1.3 copy-done.5
  457.9 3.0 fusion.19
  460.9 1.3 copy-done.2
  462.2 3.1 fusion.20
  465.7 1.7 copy.36
  467.8 1.7 copy.38
  469.6 17.5 %reduce-scatter.9.cloned.1.call-done = f32[48,512]{1,0:T(8,128)} async-done(((f32[384,512]{1,0:T(8,128)}), f32[48,512]{1,0:T(8,128)}) %reduce-scatter.9.cloned.1.call-update) | async-done | bytes 98320 | tf_op jit(solution)/shard_map/reduce_scatter | solution.py:55
  487.1 1.5 convert_element_type.96
  488.6 37.9 %reduce-scatter.11.cloned.1.call-done = f32[48,512]{1,0:T(8,128)} async-done(((f32[384,512]{1,0:T(8,128)}), f32[48,512]{1,0:T(8,128)}) %reduce-scatter.11.cloned.1.call-update) | async-done | bytes 98320 | tf_op jit(solution)/shard_map/reduce_scatter | solution.py:78
  526.5 1.1 fusion.10
  527.5 33.1 %psum.22 = f32[48]{0:T(128)S(1)} all-reduce(f32[48]{0:T(128)S(1)} %get-tuple-element.7), channel_id=1, replica_groups=mesh['dp'=2,'row'=16,'col'=8] {'row'}, use_global_device_ids=true, to_apply=%region_7.0 | all-reduce | flops 48 | bytes 384 | tf_op jit(solution)/shard_map/psum | solution.py:103
  560.6 40.5 %psum.23 = f32[512]{0:T(512)} all-reduce(f32[512]{0:T(512)S(1)} %get-tuple-element.6), channel_id=1, replica_groups=mesh['dp'=2,'row'=16,'col'=8] {'dp','col'}, use_global_device_ids=true, to_apply=%region_9.0 | all-reduce | flops 512 | bytes 4096 | tf_op jit(solution)/shard_map/psum | solution.py:102
  601.1 1.6 fusion.6
  602.7 3.6 mul.141
  606.3 2.9 mul.142
  609.3 1.1 broadcast_in_dim.52
  610.8 1.6 bitcast_multiply_fusion
  (82 shorter events, 3.0 us)
Async XLA Ops:
  7.2 65.7 %all-gather.7.cloned.1.call-start = ((), (), s32[]{:S(2)}) async-start(), calls=%async_computation.6 | async-start | bytes 2752512 | tf_op jit(solution)/shard_map/all_gather | solution.py:29
  9.6 1.1 copy-start.14
  9.6 1.5 copy-start.6
  10.7 64.7 %all-gather.9.cloned.1.call-start = ((), (), s32[]{:S(2)}) async-start(), calls=%async_computation.7 | async-start | bytes 2752512 | tf_op jit(solution)/shard_map/all_gather | solution.py:30
  11.7 1.1 copy-start.15
  11.7 2.4 copy-start.7
  12.7 88.6 %all-gather.13.cloned.1.call-start = ((), (), s32[]{:S(2)}) async-start(), calls=%async_computation.9 | async-start | bytes 2752512 | tf_op jit(solution)/shard_map/all_gather | solution.py:32
  14.1 1.2 copy-start.8
  14.1 36.1 %copy-start.11 = (f32[512]{0:T(512)S(1)}, f32[512]{0:T(512)}, u32[]{:S(2)}) copy-start(f32[512]{0:T(512)} %param.10) | copy-start | bytes 6148
  15.2 198.7 %all-reduce.4.cloned.1.call-start = ((), (), s32[]{:S(2)}) async-start(), calls=%async_computation.17 | async-start | bytes 11010048
  49.6 0.6 copy-start.12
  80.9 0.8 copy-start.10
  81.0 216.0 %reduce-scatter.19.cloned.1.call-start = ((), (), s32[]{:S(2)}) async-start(), calls=%async_computation.18 | async-start | bytes 2924544
  106.2 0.7 copy-start.16
  106.2 241.1 %copy-start.1 = (bf16[1792,512]{1,0:T(8,128)(2,1)S(1)}, bf16[1792,512]{1,0:T(8,128)(2,1)}, u32[]{:S(2)}) copy-start(bf16[1792,512]{1,0:T(8,128)(2,1)} %all-gather.13.cloned.1.call-done) | copy-start | bytes 5505028
  106.2 241.1 %all-gather.11.cloned.1.call-start = ((), (), s32[]{:S(2)}) async-start(), calls=%async_computation.8 | async-start | bytes 1462272 | tf_op jit(solution)/shard_map/all_gather | solution.py:53
  298.9 99.3 %all-gather.15.cloned.1.call-start = ((), (), s32[]{:S(2)}) async-start(), calls=%async_computation.11 | async-start | bytes 1462272 | tf_op jit(solution)/shard_map/all_gather | solution.py:75
  299.6 149.4 %all-gather.17.cloned.1.call-start = ((), (), s32[]{:S(2)}) async-start(), calls=%async_computation.12 | async-start | bytes 1462272 | tf_op jit(solution)/shard_map/all_gather | solution.py:76
  300.4 186.7 %reduce-scatter.9.cloned.1.call-start = ((), (), s32[]{:S(2)}) async-start(), calls=%async_computation.10 | async-start | bytes 884736 | tf_op jit(solution)/shard_map/reduce_scatter | solution.py:55
  350.5 98.6 %copy-start.3 = (bf16[512,1792]{0,1:T(8,128)(2,1)S(1)}, bf16[512,1792]{0,1:T(8,128)(2,1)}, u32[]{:S(2)}) copy-start(bf16[512,1792]{0,1:T(8,128)(2,1)} %all-gather.9.cloned.1.call-done) | copy-start | bytes 5505028
  350.5 176.0 %reduce-scatter.11.cloned.1.call-start = ((), (), s32[]{:S(2)}) async-start(), calls=%async_computation.13 | async-start | bytes 884736 | tf_op jit(solution)/shard_map/reduce_scatter | solution.py:78
  452.2 150.5 %reduce-scatter.13.cloned.1.call-start = ((), (), s32[]{:S(2)}) async-start(), calls=%async_computation.14 | async-start | bytes 5505024 | tf_op jit(solution)/shard_map/reduce_scatter | solution.py:95
  456.5 1.3 copy-start.5
  456.6 149.8 %reduce-scatter.15.cloned.1.call-start = ((), (), s32[]{:S(2)}) async-start(), calls=%async_computation.15 | async-start | bytes 5505024 | tf_op jit(solution)/shard_map/reduce_scatter | solution.py:96
  460.9 1.3 copy-start.2
  460.9 148.4 %reduce-scatter.17.cloned.1.call-start = ((), (), s32[]{:S(2)}) async-start(), calls=%async_computation.16 | async-start | bytes 5505024 | tf_op jit(solution)/shard_map/reduce_scatter | solution.py:98
  467.8 58.7 %copy-start.9 = (bf16[48,512]{1,0:T(8,128)(2,1)S(1)}, bf16[48,512]{1,0:T(8,128)(2,1)}, u32[]{:S(2)}) copy-start(bf16[48,512]{1,0:T(8,128)(2,1)} %param.9) | copy-start | bytes 147460
  467.8 58.7 %copy-start.13 = (f32[48]{0:T(128)S(1)}, f32[48]{0:T(128)}, u32[]{:S(2)}) copy-start(f32[48]{0:T(128)} %copy-done.12) | copy-start | bytes 580
  602.7 3.6 copy-start
  609.3 1.5 copy-start.4
Sparse Core Ops, SparseCore 0:
  10.8 20.0 all-gather.6
  33.2 16.8 all-gather.8
  52.5 16.8 all-gather.12
  81.1 132.8 all-reduce.3
  217.4 79.5 reduce-scatter.18
  299.9 47.4 all-gather.10
  350.4 47.7 all-gather.14
  401.3 47.7 all-gather.16
  452.2 34.8 reduce-scatter.8
  489.5 36.9 reduce-scatter.10
  529.0 20.7 reduce-scatter.12
  552.1 18.3 reduce-scatter.14
  573.0 18.6 reduce-scatter.16
where the time goes:
time: 620 us; the launch traced here: 619 us
  waiting for transfers between devices  388 us (63%)
  blocking collectives  150 us (24%)
  matrix products  26.8 us (4%)
  other arithmetic  21.5 us (3%)
  local copies, waits for them, and re-layouts  17 us (3%)
  between operations  14.8 us (2%)
    unnamed x15, waiting for transfers between devices  190 us
    all_gather x1, waiting for transfers between devices, on_device(): lax.all_gather(up_grad, 'row', axis=0, tiled=True)  48.1 us
    all_gather x1, waiting for transfers between devices, on_device(): lax.all_gather(gate_grad, 'row', axis=0, tiled=True)  47.7 us
    all_gather x1, waiting for transfers between devices, on_device(): lax.all_gather(activate(gate_part, up_part), 'row', axis=0, tiled=True)  46.9 us
    psum x1, blocking collectives, on_device(): lax.psum(jnp.sum(normed_grad * token_f * inv_rms, axis=0), ('dp', 'col'))  40.5 us
    reduce_scatter x1, waiting for transfers between devices, on_device(): lax.psum_scatter(lax.dot_general(gate_grads, gate_full, contract_last, pr...  37.9 us
    psum x1, blocking collectives, on_device(): square = lax.psum(jnp.sum(token_f * token_f, axis=1), 'row')  34.2 us
    psum x1, blocking collectives, on_device(): lax.psum(jnp.sum(norm_gain * normed_grad * token_f, axis=1), 'row')  33.1 us
  transfers between devices with their start and end apart: 13, of which 7 were waited for; matrix products, arithmetic and copies ran while one was open for 8% of the time, Pallas kernels for 0%

commit v1 on v0

--- a/solution.py
+++ b/solution.py
@@ -73,7 +73,9 @@
     up_grad = (hidden_grad * gate_part * sigmoid_gate).astype(jnp.bfloat16)
     gate_grads, up_grads = (
         lax.all_gather(gate_grad, "row", axis=0, tiled=True),
-        lax.all_gather(up_grad, "row", axis=0, tiled=True),
+        jnp.concatenate(
+            lax.all_to_all(jnp.stack([up_grad] * lax.axis_size("row")), "row", 0, 0), axis=0
+        ),
     )
     normed_grad = lax.psum_scatter(
         lax.dot_general(gate_grads, gate_full, contract_last, preferred_element_type=jnp.float32)

time: 620 us -> 575 us (0.927)
  waiting for transfers between devices: 388 us -> 338 us
    all_gather x1 -> x0, waiting for transfers between devices: 48.1 us -> none  [on_device(): lax.all_gather(up_grad, 'row', axis=0, tiled=True)]
    unnamed x15 -> x14, waiting for transfers between devices: 190 us -> 190 us
  transfers between devices with their start and end apart: 13 -> 13, of which waited for: 7 -> 6; matrix products, arithmetic and copies ran while one was open for 8% -> 9% of each run, Pallas kernels for 0% -> 0%
where the time goes in v1:
time: 575 us; the launch traced here: 574 us
  waiting for transfers between devices  338 us (59%)
  blocking collectives  150 us (26%)
  matrix products  26.1 us (5%)
  other arithmetic  21.5 us (4%)
  local copies, waits for them, and re-layouts  18.2 us (3%)
  between operations  15.1 us (3%)
    unnamed x14, waiting for transfers between devices  190 us
    all_gather x1, waiting for transfers between devices, on_device(): lax.all_gather(activate(gate_part, up_part), 'row', axis=0, tiled=True)  47.3 us
    all_gather x1, waiting for transfers between devices, on_device(): lax.all_gather(gate_grad, 'row', axis=0, tiled=True)  47.1 us
    psum x1, blocking collectives, on_device(): lax.psum(jnp.sum(normed_grad * token_f * inv_rms, axis=0), ('dp', 'col'))  40.6 us
    reduce_scatter x1, waiting for transfers between devices, on_device(): lax.psum_scatter(lax.dot_general(gate_grads, gate_full, contract_last, pr...  38 us
    psum x1, blocking collectives, on_device(): square = lax.psum(jnp.sum(token_f * token_f, axis=1), 'row')  34.2 us
    psum x1, blocking collectives, on_device(): lax.psum(jnp.sum(norm_gain * normed_grad * token_f, axis=1), 'row')  33.1 us
    all_gather x1, blocking collectives, on_device(): seen_rows = lax.all_gather(normed, 'col', axis=0, tiled=True)  22.6 us
  transfers between devices with their start and end apart: 13, of which 6 were waited for; matrix products, arithmetic and copies ran while one was open for 9% of the time, Pallas kernels for 0%

profile of v1, /device:TPU:1, one launch (start us, length us, event | category | flops | bytes accessed | tf_op | source)
XLA Modules:
  0.0 573.8 jit_solution(18029155657272158399)
XLA Ops:
  7.2 0.8 fusion.13
  8.2 1.5 copy.30
  9.7 1.0 bitcast_multiply_fusion.3
  11.2 0.5 copy.32
  11.7 1.0 bitcast_multiply_fusion.2
  12.9 1.1 broadcast_in_dim.46
  14.1 1.1 bitcast_multiply_fusion.1
  15.4 34.2 %psum.21 = f32[48]{0:T(128)S(1)} all-reduce(f32[48]{0:T(128)S(1)} %fusion.7), channel_id=1, replica_groups=mesh['dp'=2,'row'=16,'col'=8] {'row'}, use_global_device_ids=true, to_apply=%region_1.0 | all-reduce | flops 48 | bytes 384 | tf_op jit(solution)/shard_map/psum | solution.py:22
  49.6 0.6 copy-done.10
  50.3 22.6 %all_gather.21 = bf16[384,512]{1,0:T(8,128)(2,1)S(1)} all-gather(bf16[48,512]{1,0:T(8,128)(2,1)S(1)} %fusion.2), channel_id=1, replica_groups=mesh['dp'=2,'row'=16,'col'=8] {'col'}, dimensions={0}, use_global_device_ids=true | all-gather | bytes 442368 | tf_op jit(solution)/shard_map/all_gather | solution.py:33
  72.9 2.4 fusion.14
  75.3 2.4 fusion.15
  77.8 3.2 pad_maximum_fusion
  81.0 0.7 copy-done.8
  81.7 19.6 %all_gather.26 = bf16[384,512]{1,0:T(8,128)(2,1)S(1)} all-gather(bf16[48,512]{1,0:T(8,128)(2,1)S(1)} %copy-done.8), channel_id=1, replica_groups=mesh['dp'=2,'row'=16,'col'=8] {'col'}, dimensions={0}, use_global_device_ids=true | all-gather | bytes 442368 | tf_op jit(solution)/shard_map/all_gather | solution.py:34
  101.3 2.6 convolution_bitcast_fusion
  103.9 2.3 copy.34
  106.4 0.6 copy-done.14
  107.0 0.6 dynamic-slice
  108.2 105.7 %all-reduce.4.cloned.1.call-done = f32[384,3584]{1,0:T(8,128)} async-done(((f32[384,3584]{1,0:T(8,128)}), f32[384,3584]{1,0:T(8,128)}) %all-reduce.4.cloned.1.call-update) | async-done | bytes 5505040
  213.9 83.0 %reduce-scatter.19.cloned.1.call-done = f32[24,1792]{1,0:T(8,128)} async-done(((f32[384,1792]{1,0:T(8,128)}), f32[24,1792]{1,0:T(8,128)}) %reduce-scatter.19.cloned.1.call-update) | async-done | bytes 172048
  297.0 1.9 multiply_convert_fusion
  298.9 0.7 all-gather.14.cloned.1.call-update
  299.6 1.2 stack.2
  300.8 4.4 all-to-all-start
  305.2 47.3 %all-gather.10.cloned.1.call-done = bf16[384,1792]{1,0:T(8,128)(2,1)} async-done(((bf16[24,1792]{1,0:T(8,128)(2,1)}), bf16[384,1792]{1,0:T(8,128)(2,1)}) %all-gather.10.cloned.1.call-update) | async-done | bytes 1376272 | tf_op jit(solution)/shard_map/all_gather | solution.py:53
  352.5 3.7 fusion.16
  356.3 47.1 %all-gather.14.cloned.1.call-done = bf16[384,1792]{1,0:T(8,128)(2,1)} async-done(((bf16[24,1792]{1,0:T(8,128)(2,1)}), bf16[384,1792]{1,0:T(8,128)(2,1)}) %all-gather.14.cloned.1.call-update) | async-done | bytes 1376272 | tf_op jit(solution)/shard_map/all_gather | solution.py:75
  403.4 2.8 fusion.17
  406.2 3.3 convolution_add_fusion
  409.6 2.9 fusion.19
  412.6 1.3 copy-done.3
  413.8 3.0 fusion.18
  416.9 1.3 copy-done.1
  418.1 3.1 fusion.20
  421.6 1.7 copy.38
  423.8 1.7 copy.36
  425.5 15.9 %reduce-scatter.9.cloned.1.call-done = f32[48,512]{1,0:T(8,128)} async-done(((f32[384,512]{1,0:T(8,128)}), f32[48,512]{1,0:T(8,128)}) %reduce-scatter.9.cloned.1.call-update) | async-done | bytes 98320 | tf_op jit(solution)/shard_map/reduce_scatter | solution.py:55
  441.4 1.5 convert_element_type.96
  442.9 38.0 %reduce-scatter.11.cloned.1.call-done = f32[48,512]{1,0:T(8,128)} async-done(((f32[384,512]{1,0:T(8,128)}), f32[48,512]{1,0:T(8,128)}) %reduce-scatter.11.cloned.1.call-update) | async-done | bytes 98320 | tf_op jit(solution)/shard_map/reduce_scatter | solution.py:80
  480.9 1.1 fusion.10
  482.0 33.1 %psum.22 = f32[48]{0:T(128)S(1)} all-reduce(f32[48]{0:T(128)S(1)} %get-tuple-element.7), channel_id=1, replica_groups=mesh['dp'=2,'row'=16,'col'=8] {'row'}, use_global_device_ids=true, to_apply=%region_7.0 | all-reduce | flops 48 | bytes 384 | tf_op jit(solution)/shard_map/psum | solution.py:105
  515.1 40.6 %psum.23 = f32[512]{0:T(512)} all-reduce(f32[512]{0:T(512)S(1)} %get-tuple-element.6), channel_id=1, replica_groups=mesh['dp'=2,'row'=16,'col'=8] {'dp','col'}, use_global_device_ids=true, to_apply=%region_9.0 | all-reduce | flops 512 | bytes 4096 | tf_op jit(solution)/shard_map/psum | solution.py:104
  555.7 1.6 fusion.6
  557.3 3.6 mul.142
  560.9 2.9 mul.141
  563.9 1.1 broadcast_in_dim.52
  565.3 1.6 bitcast_multiply_fusion
  (78 shorter events, 3.0 us)
Async XLA Ops:
  7.2 65.7 %all-gather.6.cloned.1.call-start = ((), (), s32[]{:S(2)}) async-start(), calls=%async_computation.7 | async-start | bytes 2752512 | tf_op jit(solution)/shard_map/all_gather | solution.py:29
  9.6 1.1 copy-start.12
  9.6 1.5 copy-start.4
  10.7 64.7 %all-gather.8.cloned.1.call-start = ((), (), s32[]{:S(2)}) async-start(), calls=%async_computation.8 | async-start | bytes 2752512 | tf_op jit(solution)/shard_map/all_gather | solution.py:30
  11.7 1.1 copy-start.13
  11.7 2.4 copy-start.5
  12.7 88.6 %all-gather.12.cloned.1.call-start = ((), (), s32[]{:S(2)}) async-start(), calls=%async_computation.10 | async-start | bytes 2752512 | tf_op jit(solution)/shard_map/all_gather | solution.py:32
  14.1 1.2 copy-start.6
  14.1 36.1 %copy-start.9 = (f32[512]{0:T(512)S(1)}, f32[512]{0:T(512)}, u32[]{:S(2)}) copy-start(f32[512]{0:T(512)} %param.10) | copy-start | bytes 6148
  15.2 198.7 %all-reduce.4.cloned.1.call-start = ((), (), s32[]{:S(2)}) async-start(), calls=%async_computation.17 | async-start | bytes 11010048
  49.6 0.6 copy-start.10
  80.9 0.8 copy-start.8
  81.0 216.0 %reduce-scatter.19.cloned.1.call-start = ((), (), s32[]{:S(2)}) async-start(), calls=%async_computation.18 | async-start | bytes 2924544
  106.3 0.7 copy-start.14
  106.3 246.2 %all-gather.10.cloned.1.call-start = ((), (), s32[]{:S(2)}) async-start(), calls=%async_computation.9 | async-start | bytes 1462272 | tf_op jit(solution)/shard_map/all_gather | solution.py:53
  298.9 104.6 %all-gather.14.cloned.1.call-start = ((), (), s32[]{:S(2)}) async-start(), calls=%async_computation.12 | async-start | bytes 1462272 | tf_op jit(solution)/shard_map/all_gather | solution.py:75
  300.8 105.4 %all-to-all-start = ((bf16[16,24,1792]{2,1,0:T(8,128)(2,1)}), bf16[16,24,1792]{2,1,0:T(8,128)(2,1)S(1)}, u32[]{:S(2)}, u32[]{:S(2)}) async-start(bf16[16,24,1792]{2,1,0:T(8,128)(2,1)} %stack.2), calls=%async_computation.1 | async-start | bytes 2752512 | tf_op jit(solution)/shard_map/all_to_all | solution.py:77
  305.2 136.2 %reduce-scatter.9.cloned.1.call-start = ((), (), s32[]{:S(2)}) async-start(), calls=%async_computation.11 | async-start | bytes 884736 | tf_op jit(solution)/shard_map/reduce_scatter | solution.py:55
  356.2 124.7 %reduce-scatter.11.cloned.1.call-start = ((), (), s32[]{:S(2)}) async-start(), calls=%async_computation.13 | async-start | bytes 884736 | tf_op jit(solution)/shard_map/reduce_scatter | solution.py:80
  409.5 147.8 %reduce-scatter.15.cloned.1.call-start = ((), (), s32[]{:S(2)}) async-start(), calls=%async_computation.15 | async-start | bytes 5505024 | tf_op jit(solution)/shard_map/reduce_scatter | solution.py:98
  412.5 1.3 copy-start.3
  412.5 148.4 %reduce-scatter.13.cloned.1.call-start = ((), (), s32[]{:S(2)}) async-start(), calls=%async_computation.14 | async-start | bytes 5505024 | tf_op jit(solution)/shard_map/reduce_scatter | solution.py:97
  416.8 1.3 copy-start.1
  416.8 147.0 %reduce-scatter.17.cloned.1.call-start = ((), (), s32[]{:S(2)}) async-start(), calls=%async_computation.16 | async-start | bytes 5505024 | tf_op jit(solution)/shard_map/reduce_scatter | solution.py:100
  423.7 57.2 %copy-start.7 = (bf16[48,512]{1,0:T(8,128)(2,1)S(1)}, bf16[48,512]{1,0:T(8,128)(2,1)}, u32[]{:S(2)}) copy-start(bf16[48,512]{1,0:T(8,128)(2,1)} %param.9) | copy-start | bytes 147460
  423.7 57.2 %copy-start.11 = (f32[48]{0:T(128)S(1)}, f32[48]{0:T(128)}, u32[]{:S(2)}) copy-start(f32[48]{0:T(128)} %copy-done.10) | copy-start | bytes 580
  557.3 3.6 copy-start
  563.8 1.5 copy-start.2
Sparse Core Ops, SparseCore 0:
  10.8 20.0 all-gather.5
  33.2 16.8 all-gather.7
  52.5 16.8 all-gather.11
  81.1 132.7 all-reduce.3
  217.4 79.5 reduce-scatter.18
  299.9 52.6 all-gather.9
  355.6 47.7 all-gather.13
  406.5 34.8 reduce-scatter.8
  443.9 36.9 reduce-scatter.10
  483.3 20.7 reduce-scatter.14
  506.5 18.3 reduce-scatter.12
  527.3 18.6 reduce-scatter.16
